TPU v7x, 32 devices: a whole 2x2x4 slice. The times are simulated.
32 devices in a mesh: member: 8 (over y, x, core), band: 4 (over z).
Axes of the slice: x: 2, y: 2, z: 4, core: 2. Of those that a mesh axis runs over, the one named last changes fastest.
Arguments:
- controls: float32 [16, 16, 256, 512], P('member', None, 'band'), may hold values from -6 to 6
- members: float32 [16, 16, 256, 512], P('member', None, 'band'), may hold values from -6 to 6
- loc_lon: float32 [512, 512], replicated, may hold values from -0.25 to 0.25
- loc_lat: float32 [256, 256], replicated, may hold values from -0.375 to 0.375
- balance: float32 [5, 1024, 2048], P(None, 'band', 'member'), may hold values from -1 to 1
- innovation: float32 [16, 1024, 2048], P(None, 'band', 'member'), may hold values from -6 to 6
- obs_weight: float32 [16, 1024, 2048], P(None, 'band', 'member'), may hold values from 0.2 to 5
Outputs:
- gradient: float32 [16, 16, 256, 512], P('member', None, 'band')
All inputs are finite; a program needn't handle non-finite values.
Results may differ from a plain program's by a relative error of at most 0.00012.
Values sent between devices are 32-bit elements; how exact they have to be, the bound alone decides.
No kernel may reach another device: no remote copies, remote signals or barrier semaphores. Data moves between devices by JAX's collectives and lax.ppermute only.
A program may use at most 128 MiB of HBM per device.

v0:
```python
import math
import jax
import jax.numpy as jnp
from jax import lax
from jax.sharding import PartitionSpec as P

phase_fraction = (0.625, 0.875, 0.125, 0.375)
phase_start = (0, 0, 1, 1)


def with_halo(value, sides, width, wrap):
    for axis, dim in sides:
        size, length = (lax.axis_size(axis), value.shape[dim])
        up = [(i, (i + 1) % size) for i in range(size if wrap else size - 1)]
        down = [(j, i) for i, j in up]
        last = lax.slice_in_dim(value, length - width, length, axis=dim)
        leading = lax.slice_in_dim(value, 0, width, axis=dim)
        before = lax.ppermute(last, axis, up)
        after = lax.ppermute(leading, axis, down)
        value = jnp.concatenate([before, value, after], axis=dim)
    return value


def passed_along(value, axis, by):
    length = lax.axis_size(axis)
    return lax.ppermute(value, axis, [(i, (i + by) % length) for i in range(length)])


def from_behind(value, axis, steps):
    count = lax.axis_size(axis)
    leading, last = (max(0, -steps), min(count, count - steps))
    return lax.ppermute(value, axis, [(source, source + steps) for source in range(leading, last)])


def cubic_weights(fraction):
    return (
        (-(fraction**3) + 2 * fraction**2 - fraction) / 2,
        (3 * fraction**3 - 5 * fraction**2 + 2) / 2,
        (-3 * fraction**3 + 4 * fraction**2 + fraction) / 2,
        (fraction**3 - fraction**2) / 2,
    )


def refine(padded, dim_index):
    length = padded.shape[dim_index] - 4
    phase_rows = []
    for phase_index in range(4):
        weights = cubic_weights(phase_fraction[phase_index])
        summed = jnp.zeros_like(lax.slice_in_dim(padded, 0, length, axis=dim_index))
        for tap_index in range(4):
            first = phase_start[phase_index] + tap_index
            summed = summed + weights[tap_index] * lax.slice_in_dim(
                padded, first, first + length, axis=dim_index
            )
        phase_rows.append(summed)
    stacked = jnp.stack(phase_rows, axis=dim_index + 1)
    new_shape = list(padded.shape)
    new_shape[dim_index] = 4 * length
    return stacked.reshape(new_shape)


def refine_both(padded):
    return refine(refine(padded, 1), 2)


def body(controls, members, loc_lon, loc_lat, balance, innovation, obs_weight):
    highest = lax.Precision.HIGHEST
    member_scale = 1.0 / math.sqrt(controls.shape[0] * lax.axis_size("member") - 1)
    full_lon = loc_lon.shape[0]
    stripe_width = full_lon // lax.axis_size("member")
    level_ctrl, level_members = (
        lax.all_to_all(controls, "band", split_axis=1, concat_axis=2, tiled=True),
        lax.all_to_all(members, "band", split_axis=1, concat_axis=2, tiled=True),
    )
    rowwise = jnp.einsum("klyx,ux->klyu", level_ctrl, loc_lon, precision=highest)
    fields = jnp.einsum("vy,klyx->klvx", loc_lat, rowwise, precision=highest)
    partial_value = jnp.sum(level_members * fields, axis=0) * member_scale
    summed = lax.psum(partial_value, "member")
    summed = lax.all_to_all(summed, "band", split_axis=1, concat_axis=0, tiled=True)
    wrapped = jnp.concatenate([summed[:, :, -2:], summed, summed[:, :, :2]], axis=2)
    extended = lax.dynamic_slice_in_dim(
        wrapped, lax.axis_index("member") * stripe_width, stripe_width + 4, 2
    )
    padded = with_halo(extended, (("band", 1),), 2, False)
    fine_field = refine_both(padded)
    grown_field = with_halo(fine_field, (("member", 2),), 1, True)
    grown_field = with_halo(grown_field, (("band", 1),), 1, False)
    balanced = (
        balance[0] * fine_field
        + balance[1] * grown_field[:, 1:-1, 2:]
        + balance[2] * grown_field[:, 1:-1, :-2]
        + balance[3] * grown_field[:, 2:, 1:-1]
        + balance[4] * grown_field[:, :-2, 1:-1]
    )
    weighted_misfit = obs_weight * (balanced - innovation)
    pieces = balance[1:, None] * weighted_misfit[None]
    spread = with_halo(pieces, (("member", 3),), 1, True)
    spread = with_halo(spread, (("band", 2),), 1, False)
    fine_grad = (
        balance[0] * weighted_misfit
        + spread[0][:, 1:-1, :-2]
        + spread[1][:, 1:-1, 2:]
        + spread[2][:, :-2, 1:-1]
        + spread[3][:, 2:, 1:-1]
    )
    unused, pullback = jax.vjp(refine_both, padded)
    coarse_ext = pullback(fine_grad)[0]
    west_rim = passed_along(coarse_ext[:, :, :2], "member", -1)
    east_rim = passed_along(coarse_ext[:, :, -2:], "member", 1)
    core_sum = coarse_ext[:, :, 2:-2]
    core_sum = core_sum.at[:, :, -2:].add(west_rim)
    core_sum = core_sum.at[:, :, :2].add(east_rim)
    south_rim = from_behind(core_sum[:, :2], "band", -1)
    north_rim = from_behind(core_sum[:, -2:], "band", 1)
    coarse_grad = core_sum[:, 2:-2]
    coarse_grad = coarse_grad.at[:, -2:].add(south_rim)
    coarse_grad = coarse_grad.at[:, :2].add(north_rim)
    level_grad = lax.all_to_all(coarse_grad, "band", split_axis=0, concat_axis=1, tiled=True)
    weighted = (
        level_members
        * lax.all_gather(level_grad, "member", axis=2, tiled=True)[None]
        * member_scale
    )
    adjoint = jnp.einsum("klyu,ux->klyx", weighted, loc_lon, precision=highest)
    adjoint = jnp.einsum("vy,klvx->klyx", loc_lat, adjoint, precision=highest)
    adjoint = lax.all_to_all(adjoint, "band", split_axis=2, concat_axis=1, tiled=True)
    return controls + adjoint


def solution(mesh):
    return jax.shard_map(
        body,
        mesh=mesh,
        in_specs=(
            P("member", None, "band", None),
            P("member", None, "band", None),
            P(),
            P(),
            P(None, "band", "member"),
            P(None, "band", "member"),
            P(None, "band", "member"),
        ),
        out_specs=P("member", None, "band", None),
        check_vma=False,
    )
```

profile of v0, /device:TPU:0, one launch (start us, length us, event | category | flops | bytes accessed | tf_op | source)
XLA Modules:
  0.0 769.8 jit_solution(10708017313778358526)
XLA Ops:
  11.5 6.3 all-to-all-start
  22.8 88.5 %all-to-all-done = f32[2,16,64,512]{3,2,0,1:T(8,128)} async-done(((f32[2,16,64,512]{3,2,0,1:T(8,128)}), f32[2,16,64,512]{3,2,0,1:T(8,128)}, u32[]{:S(2)}, u32[]{:S(2)}) %all-to-all-start) | async-done | bytes 4194336 | tf_op jit(solution)/shard_map/all_to_all | solution.py:73
  126.4 82.4 %all-to-all-done.1 = f32[2,16,64,512]{3,2,0,1:T(8,128)} async-done(((f32[2,16,64,512]{3,2,0,1:T(8,128)}), f32[2,16,64,512]{3,2,0,1:T(8,128)}, u32[]{:S(2)}, u32[]{:S(2)}) %all-to-all-start.1) | async-done | bytes 4194336 | tf_op jit(solution)/shard_map/all_to_all | solution.py:72
  211.6 7.2 fusion.20
  224.4 61.1 %all-reduce.34.cloned.1.call-done = f32[4,256,512]{1,2,0:T(8,128)} async-done(((f32[4,256,512]{1,2,0:T(8,128)}), f32[4,256,512]{1,2,0:T(8,128)}) %all-reduce.34.cloned.1.call-update) | async-done | bytes 2097168 | tf_op jit(solution)/shard_map/psum | solution.py:78
  293.3 46.9 %all-to-all-done.2 = f32[4,256,512]{2,0,1:T(4,128)S(1)} async-done(((f32[4,256,512]{2,0,1:T(4,128)}), f32[4,256,512]{2,0,1:T(4,128)S(1)}, u32[]{:S(2)}, u32[]{:S(2)}) %all-to-all-start.2) | async-done | bytes 2097184 | tf_op jit(solution)/shard_map/all_to_all | solution.py:79
  357.1 8.6 %copy.114 = f32[16,256,64,4]{1,0,3,2:T(8,128)} copy(f32[16,256,64,4]{2,0,1,3:T(8,128)} %pad_maximum_fusion.2) | data formatting | bytes 8388608 | tf_op jit(solution)/shard_map/stack | solution.py:56
  406.6 20.2 %fusion.3 = f32[16,256,256]{1,0,2:T(8,128)} fusion(f32[16,256,256]{1,0,2:T(8,128)} %copy.124, f32[16,256,256]{1,0,2:T(8,128)} %copy.123, f32[16,1,258]{1,0,2:T(8,128)} %copy.122, f32[16,256,1]{1,0,2:T(8,128)S(1)} %collective-permute-done.2, f32[16,256,256]{1,0,2:T(8,128)} %bitcast.240, f32[16,256,1]{1,0,2:T(8,128)S(1)} %collective-permute-done.3, ...), kind=kLoop, calls=%fused_computation.17 | loop fusion | flops 19922944 | bytes 18153728 | tf_op jit(solution)/shard_map/mul | solution.py:95
  426.8 10.8 %broadcast_multiply_fusion = f32[4,16,256,256]{2,1,3,0:T(8,128)} fusion(f32[16,256,256]{1,0,2:T(8,128)} %fusion.3, f32[4,256,256]{1,2,0:T(8,128)} %copy.125), kind=kLoop, calls=%fused_computation.3 | loop fusion | flops 4194304 | bytes 22020096 | tf_op jit(solution)/shard_map/mul | solution.py:96
  443.8 6.8 pad_maximum_fusion.1
  450.6 7.3 fusion.39
  457.9 6.5 copy.126
  467.5 6.5 copy.127
  475.5 6.4 copy.128
  481.9 6.3 copy.129
  488.2 25.8 %pad_maximum_fusion = f32[4,16,258,258]{2,1,3,0:T(8,128)} fusion(f32[4,16,1,258]{2,1,3,0:T(8,128)} %copy.129, f32[4,16,256,1]{2,1,3,0:T(8,128)S(1)} %collective-permute-done.7, f32[4,16,256,256]{2,1,3,0:T(8,128)} %broadcast_multiply_fusion, f32[4,16,256,1]{2,1,3,0:T(8,128)S(1)} %collective-permute-done.6, f32[4,16,1,258]{2,1,3,0:T(8,128)} %copy.128), kind=kLoop, calls=%fused_computation | loop fusion | flops 17040384 | bytes 34080768 | tf_op jit(solution)/shard_map/concatenate | solution.py:20
  514.1 17.6 %slice_bitcast_fusion.3 = (f32[16,258,258]{1,0,2:T(8,128)}, f32[16,258,258]{1,0,2:T(8,128)}, f32[16,258,258]{1,0,2:T(8,128)}, f32[16,258,258]{1,0,2:T(8,128)}) fusion(f32[4,16,258,258]{2,1,3,0:T(8,128)} %pad_maximum_fusion), kind=kLoop, calls=%fused_computation.7 | loop fusion | bytes 34080768 | tf_op jit(solution)/shard_map/squeeze | solution.py:101
  531.7 9.4 %slice_add_fusion = f32[16,256,256]{1,0,2:T(8,128)S(1)} fusion(f32[16,258,258]{1,0,2:T(8,128)} %get-tuple-element.56, f32[16,258,258]{1,0,2:T(8,128)} %get-tuple-element.57, f32[16,258,258]{1,0,2:T(8,128)} %get-tuple-element.58, f32[16,258,258]{1,0,2:T(8,128)} %get-tuple-element.55, f32[16,256,256]{1,0,2:T(8,128)S(1)} %copy-done.1, f32[256,256]{0,1:T(8,128)S(1)} %copy.102), kind=kLoop, calls=%fused_computation.9 | loop fusion | flops 5242880 | bytes 25427968 | tf_op jit(solution)/shard_map/add | solution.py:100
  558.5 15.6 %scatter-add.14 = f32[16,68,64]{2,0,1:T(8,128)S(1)} dynamic-update-slice(f32[16,68,64]{2,0,1:T(8,128)S(1)} %slice.339, f32[16,68,2]{2,0,1:T(8,128)S(1)} %slice_add_fusion.4, s32[]{:T(128)} %constant.132.clone.1, s32[]{:T(128)} %constant.132.clone.1, s32[]{:T(128)} %constant.145.clone.1) | dynamic-update-slice | bytes 17412 | tf_op jit(solution)/shard_map/scatter-add | solution.py:111
  574.8 7.0 scatter-add.15
  590.4 13.3 %all_to_all.90 = f32[4,1,16384]{2,1,0:T(1,128)S(1)} all-to-all(f32[4,1,16384]{2,1,0:T(1,128)S(1)} %reshape.202), channel_id=1, replica_groups=mesh['member'=8,'band'=4] {'band'}, dimensions={0} | all-to-all | bytes 524288 | tf_op jit(solution)/shard_map/all_to_all | solution.py:118
  607.2 27.2 %all-gather.2.cloned.1.call-done = f32[4,256,512]{1,2,0:T(8,128)} async-done(((f32[4,256,64]{1,2,0:T(8,128)}), f32[4,256,512]{1,2,0:T(8,128)}) %all-gather.2.cloned.1.call-update) | async-done | bytes 2097168 | tf_op jit(solution)/shard_map/all_gather | solution.py:121
  636.3 9.8 %fusion.11 = f32[2,4,256,512]{2,3,1,0:T(8,128)S(1)} fusion(f32[2,4,256,512]{3,2,1,0:T(8,128)} %bitcast.242, f32[4,256,512]{2,1,0:T(8,128)S(1)} %copy.154, f32[512,512]{1,0:T(8,128)S(1)} %copy-done), kind=kOutput, calls=%fused_computation.33 | convolution fusion | flops 6444548096 | bytes 11534336 | tf_op jit(solution)/shard_map/klyu,ux->klyx/dot_general | solution.py:124
  656.5 98.4 %all_to_all.91 = f32[2,4,256,512]{3,1,0,2:T(4,128)S(1)} all-to-all(f32[2,4,256,512]{3,1,0,2:T(4,128)} %copy.156), channel_id=1, replica_groups=mesh['member'=8,'band'=4] {'band'}, dimensions={2} | all-to-all | bytes 8388608 | tf_op jit(solution)/shard_map/all_to_all | solution.py:126
  (117 shorter events, 159.6 us)
Async XLA Ops:
  6.5 205.0 %copy-start = (f32[512,512]{1,0:T(8,128)S(1)}, f32[512,512]{1,0:T(8,128)}, u32[]{:S(2)}) copy-start(f32[512,512]{1,0:T(8,128)} %param.17) | copy-start | bytes 3145732
  11.5 99.8 %all-to-all-start = ((f32[2,16,64,512]{3,2,0,1:T(8,128)}), f32[2,16,64,512]{3,2,0,1:T(8,128)}, u32[]{:S(2)}, u32[]{:S(2)}) async-start(f32[2,16,64,512]{3,2,0,1:T(8,128)} %copy.99), calls=%async_computation | async-start | bytes 8388608 | tf_op jit(solution)/shard_map/all_to_all | solution.py:73
  111.3 97.5 %all-to-all-start.1 = ((f32[2,16,64,512]{3,2,0,1:T(8,128)}), f32[2,16,64,512]{3,2,0,1:T(8,128)}, u32[]{:S(2)}, u32[]{:S(2)}) async-start(f32[2,16,64,512]{3,2,0,1:T(8,128)} %copy.103), calls=%async_computation.1 | async-start | bytes 8388608 | tf_op jit(solution)/shard_map/all_to_all | solution.py:72
  116.2 169.3 %all-reduce.34.cloned.1.call-start = ((), (), s32[]{:S(2)}) async-start(), calls=%async_computation.5 | async-start | bytes 4194304 | tf_op jit(solution)/shard_map/psum | solution.py:78
  211.5 7.2 copy-start.3
  211.5 7.2 copy-start.4
  288.6 51.6 %all-to-all-start.2 = ((f32[4,256,512]{2,0,1:T(4,128)}), f32[4,256,512]{2,0,1:T(4,128)S(1)}, u32[]{:S(2)}, u32[]{:S(2)}) async-start(f32[4,256,512]{2,0,1:T(4,128)} %copy.108), calls=%async_computation.2 | async-start | bytes 4194304 | tf_op jit(solution)/shard_map/all_to_all | solution.py:79
  293.1 341.3 %all-gather.2.cloned.1.call-start = ((), (), s32[]{:S(2)}) async-start(), calls=%async_computation.6 | async-start | bytes 2359296 | tf_op jit(solution)/shard_map/all_gather | solution.py:121
  341.8 2.7 collective-permute-start
  343.1 5.6 collective-permute-start.1
  366.5 1.4 collective-permute-start.2
  366.5 4.1 collective-permute-start.3
  377.9 24.7 %collective-permute-start.4 = (f32[16,1,258]{2,0,1:T(8,128)S(1)}, f32[16,1,258]{2,0,1:T(8,128)S(1)}, u32[]{:S(2)}, u32[]{:S(2)}) collective-permute-start(f32[16,1,258]{2,0,1:T(8,128)S(1)} %copy.118), channel_id=1, source_target_pairs={{1,0},{2,1},{3,2},{5,4},{6,5},{7,6},{9,8},{10,9},{11,10},{13,12},{... | collective-permute-start | bytes 49544 | tf_op jit(solution)/shard_map/ppermute | solution.py:19
  380.3 23.7 %collective-permute-start.5 = (f32[16,1,258]{2,0,1:T(8,128)S(1)}, f32[16,1,258]{2,0,1:T(8,128)S(1)}, u32[]{:S(2)}, u32[]{:S(2)}) collective-permute-start(f32[16,1,258]{2,0,1:T(8,128)S(1)} %copy.121), channel_id=1, source_target_pairs={{0,1},{1,2},{2,3},{4,5},{5,6},{6,7},{8,9},{9,10},{10,11},{12,13},{... | collective-permute-start | bytes 49544 | tf_op jit(solution)/shard_map/ppermute | solution.py:18
  438.4 5.3 collective-permute-start.6
  438.5 5.3 collective-permute-start.7
  464.4 11.1 %collective-permute-start.8 = (f32[4,16,1,258]{3,1,2,0:T(8,128)S(1)}, f32[4,16,1,258]{3,1,2,0:T(8,128)S(1)}, u32[]{:S(2)}, u32[]{:S(2)}) collective-permute-start(f32[4,16,1,258]{3,1,2,0:T(8,128)S(1)} %copy.126), channel_id=1, source_target_pairs={{0,1},{1,2},{2,3},{4,5},{5,6},{6,7},{8,9},{9,10},{10,11},{12,13},{... | collective-permute-start | bytes 198152 | tf_op jit(solution)/shard_map/ppermute | solution.py:18
  474.0 7.9 %collective-permute-start.9 = (f32[4,16,1,258]{3,1,2,0:T(8,128)S(1)}, f32[4,16,1,258]{3,1,2,0:T(8,128)S(1)}, u32[]{:S(2)}, u32[]{:S(2)}) collective-permute-start(f32[4,16,1,258]{3,1,2,0:T(8,128)S(1)} %copy.127), channel_id=1, source_target_pairs={{1,0},{2,1},{3,2},{5,4},{6,5},{7,6},{9,8},{10,9},{11,10},{13,12},{... | collective-permute-start | bytes 198152 | tf_op jit(solution)/shard_map/ppermute | solution.py:19
  514.1 17.6 %copy-start.1 = (f32[16,256,256]{1,0,2:T(8,128)S(1)}, f32[16,256,256]{1,0,2:T(8,128)}, u32[]{:S(2)}) copy-start(f32[16,256,256]{1,0,2:T(8,128)} %fusion.3) | copy-start | bytes 12582916
  554.8 3.1 collective-permute-start.10
  557.0 17.4 %collective-permute-start.11 = (f32[16,68,2]{1,0,2:T(8,128)S(1)}, f32[16,68,2]{1,0,2:T(8,128)S(1)}, u32[]{:S(2)}, u32[]{:S(2)}) collective-permute-start(f32[16,68,2]{1,0,2:T(8,128)S(1)} %copy.149), channel_id=1, source_target_pairs={{0,4},{4,8},{8,12},{12,16},{16,20},{20,24},{24,28},{28,0},{1,5},{5... | collective-permute-start | bytes 26120 | tf_op jit(solution)/shard_map/ppermute | solution.py:26
  581.9 6.5 collective-permute-start.12
  583.2 6.6 collective-permute-start.13
  636.3 9.8 %copy-start.5 = (f32[256,256]{1,0:T(8,128)S(1)}, f32[256,256]{1,0:T(8,128)}, u32[]{:S(2)}) copy-start(f32[256,256]{1,0:T(8,128)} %param.18) | copy-start | bytes 786436
  (2 other events, 7.7 us)
Sparse Core Ops, SparseCore 0:
  224.5 60.9 all-reduce.33
  607.3 27.0 all-gather.1
where the time goes:
time: 780 us; the launch traced here: 770 us
  waiting for transfers between devices  319 us (41%)
  local copies, waits for them, and re-layouts  158 us (20%)
  blocking collectives  112 us (14%)
  other arithmetic  100 us (13%)
  starting transfers between devices  40.8 us (5%)
  matrix products  25.9 us (3%)
  between operations  14.3 us (2%)
    all_to_all x1, blocking collectives, body(): lax.all_to_all(adjoint, 'band', split_axis=2, concat_axis=1, tiled=True)  98.4 us
    all_to_all x1, waiting for transfers between devices, body(): lax.all_to_all(members, 'band', split_axis=1, concat_axis=2, tiled=True)  88.5 us
    all_to_all x1, waiting for transfers between devices, body(): lax.all_to_all(controls, 'band', split_axis=1, concat_axis=2, tiled=True)  82.4 us
    psum x1, waiting for transfers between devices, body(): summed = lax.psum(partial_value, 'member')  61.1 us
    all_to_all x1, waiting for transfers between devices, body(): lax.all_to_all(summed, 'band', split_axis=1, concat_axis=0, tiled=True)  46.9 us
    concatenate x3, other arithmetic, with_halo(): value = jnp.concatenate([before, value, after], axis=dim)  35.3 us
    all_gather x1, waiting for transfers between devices, body(): lax.all_gather(level_grad, 'member', axis=2, tiled=True)[None]  27.2 us
    unnamed x18, local copies, waits for them, and re-layouts  23.1 us
  transfers between devices with their start and end apart: 19, of which 12 were waited for; matrix products, arithmetic and copies ran while one was open for 8% of the time, Pallas kernels for 0%

commit v1 on v0

--- a/solution.py
+++ b/solution.py
@@ -75,7 +75,9 @@
     rowwise = jnp.einsum("klyx,ux->klyu", level_ctrl, loc_lon, precision=highest)
     fields = jnp.einsum("vy,klyx->klvx", loc_lat, rowwise, precision=highest)
     partial_value = jnp.sum(level_members * fields, axis=0) * member_scale
-    summed = lax.psum(partial_value, "member")
+    summed = partial_value
+    for hop in (1, 2, 4):
+        summed = summed + lax.ppermute(summed, "member", [(dev, dev ^ hop) for dev in range(8)])
     summed = lax.all_to_all(summed, "band", split_axis=1, concat_axis=0, tiled=True)
     wrapped = jnp.concatenate([summed[:, :, -2:], summed, summed[:, :, :2]], axis=2)
     extended = lax.dynamic_slice_in_dim(

time: 780 us -> 814 us (1.044)
  waiting for transfers between devices: 319 us -> 355 us
    ppermute x0 -> x3, waiting for transfers between devices: none -> 95.5 us  [body(): lax.ppermute(summed, 'member', [(dev, dev ^ hop) for dev in range(8)])]
    psum x1 -> x0, waiting for transfers between devices: 61.1 us -> none  [body(): summed = lax.psum(partial_value, 'member')]
  transfers between devices with their start and end apart: 19 -> 21, of which waited for: 12 -> 15; matrix products, arithmetic and copies ran while one was open for 8% -> 8% of each run, Pallas kernels for 0% -> 0%
where the time goes in v1:
time: 814 us; the launch traced here: 804 us
  waiting for transfers between devices  355 us (44%)
  local copies, waits for them, and re-layouts  157 us (19%)
  blocking collectives  113 us (14%)
  other arithmetic  99.8 us (12%)
  starting transfers between devices  38.9 us (5%)
  matrix products  25.9 us (3%)
  between operations  14.3 us (2%)
    all_to_all x1, blocking collectives, body(): lax.all_to_all(adjoint, 'band', split_axis=2, concat_axis=1, tiled=True)  98.4 us
    ppermute x3, waiting for transfers between devices, body(): lax.ppermute(summed, 'member', [(dev, dev ^ hop) for dev in range(8)])  95.5 us
    all_to_all x1, waiting for transfers between devices, body(): lax.all_to_all(members, 'band', split_axis=1, concat_axis=2, tiled=True)  88.5 us
    all_to_all x1, waiting for transfers between devices, body(): lax.all_to_all(controls, 'band', split_axis=1, concat_axis=2, tiled=True)  82.4 us
    all_to_all x1, waiting for transfers between devices, body(): lax.all_to_all(summed, 'band', split_axis=1, concat_axis=0, tiled=True)  47 us
    concatenate x3, other arithmetic, with_halo(): value = jnp.concatenate([before, value, after], axis=dim)  35.3 us
    all_gather x1, waiting for transfers between devices, body(): lax.all_gather(level_grad, 'member', axis=2, tiled=True)[None]  27.2 us
    unnamed x18, local copies, waits for them, and re-layouts  23.4 us
  transfers between devices with their start and end apart: 21, of which 15 were waited for; matrix products, arithmetic and copies ran while one was open for 8% of the time, Pallas kernels for 0%

profile of v1, /device:TPU:0, one launch (start us, length us, event | category | flops | bytes accessed | tf_op | source)
XLA Modules:
  0.0 803.8 jit_solution(13347105874040606656)
XLA Ops:
  11.5 6.3 all-to-all-start
  22.8 88.5 %all-to-all-done = f32[2,16,64,512]{3,2,0,1:T(8,128)} async-done(((f32[2,16,64,512]{3,2,0,1:T(8,128)}), f32[2,16,64,512]{3,2,0,1:T(8,128)}, u32[]{:S(2)}, u32[]{:S(2)}) %all-to-all-start) | async-done | bytes 4194336 | tf_op jit(solution)/shard_map/all_to_all | solution.py:73
  126.4 82.4 %all-to-all-done.1 = f32[2,16,64,512]{3,2,0,1:T(8,128)} async-done(((f32[2,16,64,512]{3,2,0,1:T(8,128)}), f32[2,16,64,512]{3,2,0,1:T(8,128)}, u32[]{:S(2)}, u32[]{:S(2)}) %all-to-all-start.1) | async-done | bytes 4194336 | tf_op jit(solution)/shard_map/all_to_all | solution.py:72
  211.6 7.2 fusion.20
  229.2 46.1 %collective-permute-done.1 = f32[4,256,512]{1,2,0:T(8,128)S(1)} collective-permute-done((f32[4,256,512]{1,2,0:T(8,128)S(1)}, f32[4,256,512]{1,2,0:T(8,128)S(1)}, u32[]{:S(2)}, u32[]{:S(2)}) %collective-permute-start.1) | collective-permute-done | bytes 2097184 | tf_op jit(solution)/shard_map/ppermute | solution.py:80
  277.2 45.2 %collective-permute-done.2 = f32[4,256,512]{1,2,0:T(8,128)S(1)} collective-permute-done((f32[4,256,512]{1,2,0:T(8,128)S(1)}, f32[4,256,512]{1,2,0:T(8,128)S(1)}, u32[]{:S(2)}, u32[]{:S(2)}) %collective-permute-start.2) | collective-permute-done | bytes 2097184 | tf_op jit(solution)/shard_map/ppermute | solution.py:80
  328.5 47.0 %all-to-all-done.2 = f32[4,256,512]{2,0,1:T(4,128)S(1)} async-done(((f32[4,256,512]{2,0,1:T(4,128)}), f32[4,256,512]{2,0,1:T(4,128)S(1)}, u32[]{:S(2)}, u32[]{:S(2)}) %all-to-all-start.2) | async-done | bytes 2097184 | tf_op jit(solution)/shard_map/all_to_all | solution.py:81
  392.4 8.6 %copy.114 = f32[16,256,64,4]{1,0,3,2:T(8,128)} copy(f32[16,256,64,4]{2,0,1,3:T(8,128)} %pad_maximum_fusion.2) | data formatting | bytes 8388608 | tf_op jit(solution)/shard_map/stack | solution.py:56
  441.9 20.1 %fusion.3 = f32[16,256,256]{1,0,2:T(8,128)} fusion(f32[16,256,256]{1,0,2:T(8,128)} %copy.124, f32[16,256,256]{1,0,2:T(8,128)} %copy.123, f32[16,1,258]{1,0,2:T(8,128)} %copy.122, f32[16,256,1]{1,0,2:T(8,128)S(1)} %collective-permute-done.5, f32[16,256,256]{1,0,2:T(8,128)} %bitcast.240, f32[16,256,1]{1,0,2:T(8,128)S(1)} %collective-permute-done.6, ...), kind=kLoop, calls=%fused_computation.17 | loop fusion | flops 19922944 | bytes 18153728 | tf_op jit(solution)/shard_map/mul | solution.py:97
  462.0 10.8 %broadcast_multiply_fusion = f32[4,16,256,256]{2,1,3,0:T(8,128)} fusion(f32[16,256,256]{1,0,2:T(8,128)} %fusion.3, f32[4,256,256]{1,2,0:T(8,128)} %copy.125), kind=kLoop, calls=%fused_computation.3 | loop fusion | flops 4194304 | bytes 22020096 | tf_op jit(solution)/shard_map/mul | solution.py:98
  478.4 6.8 pad_maximum_fusion.1
  485.3 7.3 fusion.40
  492.6 6.5 copy.126
  502.0 6.5 copy.127
  509.8 6.6 copy.128
  522.7 25.9 %pad_maximum_fusion = f32[4,16,258,258]{2,1,3,0:T(8,128)} fusion(f32[4,16,1,258]{2,1,3,0:T(8,128)} %copy.129, f32[4,16,256,1]{2,1,3,0:T(8,128)S(1)} %collective-permute-done.10, f32[4,16,256,256]{2,1,3,0:T(8,128)} %broadcast_multiply_fusion, f32[4,16,256,1]{2,1,3,0:T(8,128)S(1)} %collective-permute-done.9, f32[4,16,1,258]{2,1,3,0:T(8,128)} %copy.128), kind=kLoop, calls=%fused_computation | loop fusion | flops 17040384 | bytes 34080768 | tf_op jit(solution)/shard_map/concatenate | solution.py:20
  548.6 17.6 %slice_bitcast_fusion.3 = (f32[16,258,258]{1,0,2:T(8,128)}, f32[16,258,258]{1,0,2:T(8,128)}, f32[16,258,258]{1,0,2:T(8,128)}, f32[16,258,258]{1,0,2:T(8,128)}) fusion(f32[4,16,258,258]{2,1,3,0:T(8,128)} %pad_maximum_fusion), kind=kLoop, calls=%fused_computation.7 | loop fusion | bytes 34080768 | tf_op jit(solution)/shard_map/squeeze | solution.py:103
  566.2 9.4 %slice_add_fusion = f32[16,256,256]{1,0,2:T(8,128)S(1)} fusion(f32[16,258,258]{1,0,2:T(8,128)} %get-tuple-element.56, f32[16,258,258]{1,0,2:T(8,128)} %get-tuple-element.57, f32[16,258,258]{1,0,2:T(8,128)} %get-tuple-element.58, f32[16,258,258]{1,0,2:T(8,128)} %get-tuple-element.55, f32[16,256,256]{1,0,2:T(8,128)S(1)} %copy-done.1, f32[256,256]{0,1:T(8,128)S(1)} %copy.102), kind=kLoop, calls=%fused_computation.9 | loop fusion | flops 5242880 | bytes 25427968 | tf_op jit(solution)/shard_map/add | solution.py:102
  591.5 15.6 %scatter-add.14 = f32[16,68,64]{2,0,1:T(8,128)S(1)} dynamic-update-slice(f32[16,68,64]{2,0,1:T(8,128)S(1)} %slice.339, f32[16,68,2]{2,0,1:T(8,128)S(1)} %slice_add_fusion.4, s32[]{:T(128)} %constant.132.clone.1, s32[]{:T(128)} %constant.132.clone.1, s32[]{:T(128)} %constant.145.clone.1) | dynamic-update-slice | bytes 17412 | tf_op jit(solution)/shard_map/scatter-add | solution.py:113
  607.8 7.0 scatter-add.15
  623.3 14.3 %all_to_all.90 = f32[4,1,16384]{2,1,0:T(1,128)S(1)} all-to-all(f32[4,1,16384]{2,1,0:T(1,128)S(1)} %reshape.202), channel_id=1, replica_groups=mesh['member'=8,'band'=4] {'band'}, dimensions={0} | all-to-all | bytes 524288 | tf_op jit(solution)/shard_map/all_to_all | solution.py:120
  641.1 27.2 %all-gather.2.cloned.1.call-done = f32[4,256,512]{1,2,0:T(8,128)} async-done(((f32[4,256,64]{1,2,0:T(8,128)}), f32[4,256,512]{1,2,0:T(8,128)}) %all-gather.2.cloned.1.call-update) | async-done | bytes 2097168 | tf_op jit(solution)/shard_map/all_gather | solution.py:123
  670.2 9.8 %fusion.11 = f32[2,4,256,512]{2,3,1,0:T(8,128)S(1)} fusion(f32[2,4,256,512]{3,2,1,0:T(8,128)} %bitcast.242, f32[4,256,512]{2,1,0:T(8,128)S(1)} %copy.154, f32[512,512]{1,0:T(8,128)S(1)} %copy-done), kind=kOutput, calls=%fused_computation.33 | convolution fusion | flops 6444548096 | bytes 11534336 | tf_op jit(solution)/shard_map/klyu,ux->klyx/dot_general | solution.py:126
  690.4 98.4 %all_to_all.91 = f32[2,4,256,512]{3,1,0,2:T(4,128)S(1)} all-to-all(f32[2,4,256,512]{3,1,0,2:T(4,128)} %copy.156), channel_id=1, replica_groups=mesh['member'=8,'band'=4] {'band'}, dimensions={2} | all-to-all | bytes 8388608 | tf_op jit(solution)/shard_map/all_to_all | solution.py:128
  (123 shorter events, 168.3 us)
Async XLA Ops:
  6.5 205.0 %copy-start = (f32[512,512]{1,0:T(8,128)S(1)}, f32[512,512]{1,0:T(8,128)}, u32[]{:S(2)}) copy-start(f32[512,512]{1,0:T(8,128)} %param.17) | copy-start | bytes 3145732
  11.5 99.8 %all-to-all-start = ((f32[2,16,64,512]{3,2,0,1:T(8,128)}), f32[2,16,64,512]{3,2,0,1:T(8,128)}, u32[]{:S(2)}, u32[]{:S(2)}) async-start(f32[2,16,64,512]{3,2,0,1:T(8,128)} %copy.99), calls=%async_computation | async-start | bytes 8388608 | tf_op jit(solution)/shard_map/all_to_all | solution.py:73
  111.3 97.5 %all-to-all-start.1 = ((f32[2,16,64,512]{3,2,0,1:T(8,128)}), f32[2,16,64,512]{3,2,0,1:T(8,128)}, u32[]{:S(2)}, u32[]{:S(2)}) async-start(f32[2,16,64,512]{3,2,0,1:T(8,128)} %copy.103), calls=%async_computation.1 | async-start | bytes 8388608 | tf_op jit(solution)/shard_map/all_to_all | solution.py:72
  223.0 4.2 collective-permute-start
  227.5 47.7 %collective-permute-start.1 = (f32[4,256,512]{1,2,0:T(8,128)S(1)}, f32[4,256,512]{1,2,0:T(8,128)S(1)}, u32[]{:S(2)}, u32[]{:S(2)}) collective-permute-start(f32[4,256,512]{1,2,0:T(8,128)S(1)} %fusion.38), channel_id=1, source_target_pairs={{0,8},{4,12},{8,0},{12,4},{16,24},{20,28},{24,16},{28,20},{1,9},{5... | collective-permute-start | bytes 6291464 | tf_op jit(solution)/shard_map/ppermute | solution.py:80
  275.6 46.9 %collective-permute-start.2 = (f32[4,256,512]{1,2,0:T(8,128)S(1)}, f32[4,256,512]{1,2,0:T(8,128)S(1)}, u32[]{:S(2)}, u32[]{:S(2)}) collective-permute-start(f32[4,256,512]{1,2,0:T(8,128)S(1)} %add.204), channel_id=1, source_target_pairs={{0,16},{4,20},{8,24},{12,28},{16,0},{20,4},{24,8},{28,12},{1,17},{... | collective-permute-start | bytes 6291464 | tf_op jit(solution)/shard_map/ppermute | solution.py:80
  324.9 50.6 %all-to-all-start.2 = ((f32[4,256,512]{2,0,1:T(4,128)}), f32[4,256,512]{2,0,1:T(4,128)S(1)}, u32[]{:S(2)}, u32[]{:S(2)}) async-start(f32[4,256,512]{2,0,1:T(4,128)} %copy.108), calls=%async_computation.2 | async-start | bytes 4194304 | tf_op jit(solution)/shard_map/all_to_all | solution.py:81
  328.5 339.8 %all-gather.2.cloned.1.call-start = ((), (), s32[]{:S(2)}) async-start(), calls=%async_computation.5 | async-start | bytes 2359296 | tf_op jit(solution)/shard_map/all_gather | solution.py:123
  377.1 2.7 collective-permute-start.3
  378.4 5.6 collective-permute-start.4
  401.7 1.5 collective-permute-start.5
  401.8 4.2 collective-permute-start.6
  413.3 24.6 %collective-permute-start.7 = (f32[16,1,258]{2,0,1:T(8,128)S(1)}, f32[16,1,258]{2,0,1:T(8,128)S(1)}, u32[]{:S(2)}, u32[]{:S(2)}) collective-permute-start(f32[16,1,258]{2,0,1:T(8,128)S(1)} %copy.118), channel_id=1, source_target_pairs={{1,0},{2,1},{3,2},{5,4},{6,5},{7,6},{9,8},{10,9},{11,10},{13,12},{... | collective-permute-start | bytes 49544 | tf_op jit(solution)/shard_map/ppermute | solution.py:19
  415.7 23.6 %collective-permute-start.8 = (f32[16,1,258]{2,0,1:T(8,128)S(1)}, f32[16,1,258]{2,0,1:T(8,128)S(1)}, u32[]{:S(2)}, u32[]{:S(2)}) collective-permute-start(f32[16,1,258]{2,0,1:T(8,128)S(1)} %copy.121), channel_id=1, source_target_pairs={{0,1},{1,2},{2,3},{4,5},{5,6},{6,7},{8,9},{9,10},{10,11},{12,13},{... | collective-permute-start | bytes 49544 | tf_op jit(solution)/shard_map/ppermute | solution.py:18
  473.7 2.5 collective-permute-start.10
  473.8 4.6 collective-permute-start.9
  499.1 10.7 %collective-permute-start.11 = (f32[4,16,1,258]{3,1,2,0:T(8,128)S(1)}, f32[4,16,1,258]{3,1,2,0:T(8,128)S(1)}, u32[]{:S(2)}, u32[]{:S(2)}) collective-permute-start(f32[4,16,1,258]{3,1,2,0:T(8,128)S(1)} %copy.126), channel_id=1, source_target_pairs={{0,1},{1,2},{2,3},{4,5},{5,6},{6,7},{8,9},{9,10},{10,11},{12,13},{... | collective-permute-start | bytes 198152 | tf_op jit(solution)/shard_map/ppermute | solution.py:18
  508.5 7.9 collective-permute-start.12
  548.6 17.6 %copy-start.1 = (f32[16,256,256]{1,0,2:T(8,128)S(1)}, f32[16,256,256]{1,0,2:T(8,128)}, u32[]{:S(2)}) copy-start(f32[16,256,256]{1,0,2:T(8,128)} %fusion.3) | copy-start | bytes 12582916
  589.3 1.7 collective-permute-start.13
  590.0 17.4 %collective-permute-start.14 = (f32[16,68,2]{1,0,2:T(8,128)S(1)}, f32[16,68,2]{1,0,2:T(8,128)S(1)}, u32[]{:S(2)}, u32[]{:S(2)}) collective-permute-start(f32[16,68,2]{1,0,2:T(8,128)S(1)} %copy.149), channel_id=1, source_target_pairs={{0,4},{4,8},{8,12},{12,16},{16,20},{20,24},{24,28},{28,0},{1,5},{5... | collective-permute-start | bytes 26120 | tf_op jit(solution)/shard_map/ppermute | solution.py:26
  614.9 6.5 collective-permute-start.15
  616.2 6.6 collective-permute-start.16
  670.2 9.8 %copy-start.5 = (f32[256,256]{1,0:T(8,128)S(1)}, f32[256,256]{1,0:T(8,128)}, u32[]{:S(2)}) copy-start(f32[256,256]{1,0:T(8,128)} %param.18) | copy-start | bytes 786436
  (4 other events, 22.2 us)
Sparse Core Ops, SparseCore 0:
  641.2 27.0 all-gather.1
